TPU v7x, 128 devices: a whole 4x4x4 slice. The times are simulated.
128 devices in a mesh: brick: 8 (over y, core), grp: 16 (over x, z).
Axes of the slice: x: 4, y: 4, z: 4, core: 2. Of those that a mesh axis runs over, the one named last changes fastest.
Arguments:
- source: float32 [16, 8, 2, 32, 1024], P('grp', 'brick'), may hold values from -21 to 21
- uptake: float32 [16, 8, 2, 32, 1024], P('grp', 'brick'), may hold values from 0.00015 to 0.006
- conductance: float32 [16, 8, 6, 2, 32, 1024], P('grp', 'brick'), may hold values from 0 to 3, as said below
- occupancy: int32 [16, 2, 8], replicated, may hold values from 0 to 1, as said below
- assignment: int32 [8], replicated, may hold values from 0 to 7, as said below
Outputs:
- solution_field: float32 [16, 8, 2, 32, 1024], P('grp', 'brick')
- residual: float32 [16, 8, 2, 32, 1024], P('grp', 'brick')
Inputs may be any that keep to these rules, and one draw needn't show every extreme that they name: `occupancy`: 1 marks an occupied brick; in every draw one patch of some slab has all its bricks occupied. `assignment`: each patch is held by exactly one index of brick. `conductance`: equal at both ends of a bond: the value toward +x at a cell is the value toward -x at its +x neighbour, likewise for y and z, the lattice being read cyclically; values toward +z and -z are 0.3 or more.
All inputs are finite; a program needn't handle non-finite values.
Results may differ from a plain program's by a relative error of at most 0.0003.
Values sent between devices are 32-bit elements; how exact they have to be, the bound alone decides.
A program may use at most 128 MiB of HBM per device.

v0:
```python
import jax
import jax.numpy as jnp
from jax import lax
from jax.sharding import PartitionSpec as P

BS = 32
PATCH_X = 1
PATCH_Y = 2
ITERS = 3
OMEGA = 0.6


def extended_2(block, sides, width):
    for axis, dim in sides:
        count = lax.axis_size(axis)
        forward = [(i, i + 1) for i in range(count - 1)]
        backward = [(target, source) for source, target in forward]
        low = lax.ppermute(
            lax.slice_in_dim(block, block.shape[dim] - width, None, axis=dim), axis, forward
        )
        high = lax.ppermute(lax.slice_in_dim(block, 0, width, axis=dim), axis, backward)
        block = jnp.concatenate([low, block, high], axis=dim)
    return block


def assemble(coarse_diag, couplings, strides):
    extent = coarse_diag.shape[0]
    matrix = jnp.diag(coarse_diag)
    for coupling, stride in zip(couplings, strides):
        banded = coupling[: extent - stride]
        matrix = matrix - jnp.diag(banded, stride) - jnp.diag(banded, -stride)
    return matrix


def pad_rows(block, capacity):
    return jnp.pad(block, ((0, capacity - block.shape[0]), (0, 0)))


def on_device(source, uptake, conductance, occupancy, assignment):
    face_size = BS * BS
    capacity = max(PATCH_X, PATCH_Y)
    slot_count = PATCH_X * PATCH_Y
    slab_index = lax.axis_index("grp")
    brick_index = lax.axis_index("brick")
    brick_count = lax.axis_size("brick")
    across = brick_count // 2
    peer_ids = jnp.arange(brick_count, dtype=jnp.int32)
    patch_index = assignment[brick_index]
    patch_row = patch_index // across
    patch_column = patch_index % across

    def owner_of(row_shift, column_shift):
        row_target = patch_row + row_shift
        column_target = patch_column + column_shift
        inside = (
            (row_target >= 0) & (row_target < 2) & (column_target >= 0) & (column_target < across)
        )
        holder = jnp.sum(jnp.where(assignment == row_target * across + column_target, peer_ids, 0))
        return jnp.where(inside, holder, -1)

    wanted = jnp.stack([owner_of(1, 0), owner_of(-1, 0), owner_of(0, 1), owner_of(0, -1)])
    padded = jnp.pad(occupancy, 1)
    window = lax.dynamic_slice(
        padded,
        (slab_index, patch_row * PATCH_X, patch_column * PATCH_Y),
        (3, PATCH_X + 2, PATCH_Y + 2),
    ).astype(jnp.float32)
    centre = window[1, 1:-1, 1:-1].reshape(slot_count)
    toward = [
        window[1, 2:, 1:-1],
        window[1, :-2, 1:-1],
        window[1, 1:-1, 2:],
        window[1, 1:-1, :-2],
        window[2, 1:-1, 1:-1],
        window[0, 1:-1, 1:-1],
    ]
    first_axis = lax.broadcasted_iota(jnp.int32, (1, BS, face_size), 1)
    flat_axis = lax.broadcasted_iota(jnp.int32, (1, BS, face_size), 2)
    second_axis = flat_axis // BS
    third_axis = flat_axis % BS
    cube_third = lax.broadcasted_iota(jnp.int32, (1, BS, BS, BS), 3)
    borders = [
        first_axis == BS - 1,
        first_axis == 0,
        second_axis == BS - 1,
        second_axis == 0,
        third_axis == BS - 1,
        third_axis == 0,
    ]
    bonds = conductance[0, 0]
    live_here = centre[:, None, None]
    effective = []
    for direction in range(6):
        neighbour_live = toward[direction].reshape(slot_count)[:, None, None]
        active = jnp.where(borders[direction], live_here * neighbour_live, live_here)
        effective.append(bonds[direction] * active)
    absorb = uptake[0, 0]
    diagonal = absorb
    for direction in range(6):
        diagonal = diagonal + effective[direction]

    def apply_operator(field):
        lower_x = field[:, 0, :]
        upper_x = field[:, BS - 1, :]
        lower_y = field[:, :, :BS].reshape(slot_count, face_size)
        upper_y = field[:, :, face_size - BS :].reshape(slot_count, face_size)
        cube = field.reshape(slot_count, BS, BS, BS)
        lower_z = cube[:, :, :, 0].reshape(slot_count, face_size)
        upper_z = cube[:, :, :, BS - 1].reshape(slot_count, face_size)
        grid_lower_x = lower_x.reshape(PATCH_X, PATCH_Y, face_size)
        grid_upper_x = upper_x.reshape(PATCH_X, PATCH_Y, face_size)
        grid_lower_y = lower_y.reshape(PATCH_X, PATCH_Y, face_size)
        grid_upper_y = upper_y.reshape(PATCH_X, PATCH_Y, face_size)
        outgoing_sides = jnp.stack(
            [
                pad_rows(grid_lower_x[0], capacity),
                pad_rows(grid_upper_x[PATCH_X - 1], capacity),
                pad_rows(grid_lower_y[:, 0], capacity),
                pad_rows(grid_upper_y[:, PATCH_Y - 1], capacity),
            ]
        )
        portion = lax.all_gather(outgoing_sides[None], "brick", axis=0, tiled=True)
        sources = jnp.arange(portion.shape[0], dtype=jnp.int32)
        matches = sources[:, None] == wanted[None, :]
        remote = jnp.zeros((4, capacity, face_size), jnp.float32) + jnp.sum(
            jnp.where(matches[:, :, None, None], portion, 0.0), axis=0
        )
        stacked = jnp.stack([lower_z, upper_z])
        extended = extended_2(stacked, (("grp", 0),), 1)
        from_below = extended[0].reshape(slot_count, BS, BS, 1)
        from_above = extended[3].reshape(slot_count, BS, BS, 1)
        beyond_xplus = jnp.concatenate(
            [grid_lower_x[1:], remote[0, :PATCH_Y][None]], axis=0
        ).reshape(slot_count, face_size)
        beyond_xminus = jnp.concatenate(
            [remote[1, :PATCH_Y][None], grid_upper_x[:-1]], axis=0
        ).reshape(slot_count, face_size)
        beyond_yplus = jnp.concatenate(
            [grid_lower_y[:, 1:], remote[2, :PATCH_X][:, None]], axis=1
        ).reshape(slot_count, BS, BS)
        beyond_yminus = jnp.concatenate(
            [remote[3, :PATCH_X][:, None], grid_upper_y[:, :-1]], axis=1
        ).reshape(slot_count, BS, BS)
        upper_neighbour = jnp.where(
            cube_third == BS - 1, from_above, jnp.roll(cube, -1, axis=3)
        ).reshape(slot_count, BS, face_size)
        lower_neighbour = jnp.where(cube_third == 0, from_below, jnp.roll(cube, 1, axis=3)).reshape(
            slot_count, BS, face_size
        )
        total = diagonal * field
        total = total - effective[0] * jnp.concatenate(
            [field[:, 1:, :], beyond_xplus[:, None, :]], axis=1
        )
        total = total - effective[1] * jnp.concatenate(
            [beyond_xminus[:, None, :], field[:, :-1, :]], axis=1
        )
        total = total - effective[2] * jnp.concatenate([field[:, :, BS:], beyond_yplus], axis=2)
        total = total - effective[3] * jnp.concatenate(
            [beyond_yminus, field[:, :, : face_size - BS]], axis=2
        )
        total = total - effective[4] * upper_neighbour
        total = total - effective[5] * lower_neighbour
        return total

    slot_ids = jnp.arange(slot_count)
    brick_first = slot_ids // PATCH_Y
    brick_second = slot_ids % PATCH_Y
    inside = [
        (brick_first < PATCH_X - 1).astype(jnp.float32),
        (brick_first > 0).astype(jnp.float32),
        (brick_second < PATCH_Y - 1).astype(jnp.float32),
        (brick_second > 0).astype(jnp.float32),
    ]
    face_sums = [
        jnp.sum(effective[0][:, BS - 1, :], axis=1),
        jnp.sum(effective[1][:, 0, :], axis=1),
        jnp.sum(effective[2][:, :, face_size - BS :], axis=(1, 2)),
        jnp.sum(effective[3][:, :, :BS], axis=(1, 2)),
        jnp.sum(effective[4].reshape(slot_count, BS, BS, BS)[:, :, :, BS - 1], axis=(1, 2)),
        jnp.sum(effective[5].reshape(slot_count, BS, BS, BS)[:, :, :, 0], axis=(1, 2)),
    ]
    coarse_diag = jnp.sum(absorb, axis=(1, 2))
    for direction in range(4):
        coarse_diag = coarse_diag + face_sums[direction] * inside[direction]
    coarse_diag = coarse_diag + face_sums[4] + face_sums[5]
    record = jnp.stack(
        [coarse_diag, face_sums[0] * inside[0], face_sums[2] * inside[2], face_sums[4]]
    )[None]
    gathered = lax.all_gather(record, "grp", axis=0, tiled=True)
    columns = jnp.transpose(gathered, (1, 0, 2)).reshape(4, -1)
    matrix = assemble(columns[0], (columns[1], columns[2], columns[3]), (PATCH_Y, 1, slot_count))
    factor = jnp.linalg.cholesky(matrix)

    def coarse_solve(residual_field):
        totals = jnp.sum(residual_field, axis=(1, 2))
        gathered_terms = lax.all_gather(totals[None], "grp", axis=0, tiled=True).reshape(-1, 1)
        middle = lax.linalg.triangular_solve(factor, gathered_terms, left_side=True, lower=True)
        result = lax.linalg.triangular_solve(
            factor, middle, left_side=True, lower=True, transpose_a=True
        )
        return lax.dynamic_slice_in_dim(result[:, 0], slab_index * slot_count, slot_count)

    def precondition(residual_field):
        smoothed = OMEGA * residual_field / diagonal
        smoothed = smoothed + OMEGA * (residual_field - apply_operator(smoothed)) / diagonal
        return smoothed + coarse_solve(residual_field)[:, None, None]

    forcing = source[0, 0] * live_here
    solution_field = jnp.zeros_like(forcing)
    residual = forcing

    def global_sum(values):
        return lax.psum(jnp.sum(values), ("brick", "grp"))

    search = precondition(residual)
    energy = global_sum(residual * search)
    for iteration in range(ITERS):
        mapped = apply_operator(search)
        step_size = energy / global_sum(search * mapped)
        solution_field = solution_field + step_size * search
        residual = residual - step_size * mapped
        if iteration + 1 < ITERS:
            smoothed = precondition(residual)
            renewed = global_sum(residual * smoothed)
            search = smoothed + renewed / energy * search
            energy = renewed
    return (solution_field[None, None], residual[None, None])


def solution(mesh):
    return jax.shard_map(
        on_device,
        mesh=mesh,
        in_specs=(
            P("grp", "brick", None, None, None),
            P("grp", "brick", None, None, None),
            P("grp", "brick", None, None, None, None),
            P(),
            P(),
        ),
        out_specs=(P("grp", "brick", None, None, None), P("grp", "brick", None, None, None)),
        check_vma=False,
    )
```

profile of v0, /device:TPU:1, one launch (start us, length us, event | category | flops | bytes accessed | tf_op | source)
XLA Modules:
  0.0 1063.9 jit_solution(14409875242148923339)
XLA Ops:
  15.4 2.4 squeeze.120
  22.2 5.7 multiply_divide_fusion.2
  30.5 4.9 collective-permute-start.1
  45.7 14.1 %all-gather = f32[32,2,1024]{2,1,0:T(2,128)S(1)} all-gather(f32[4,2,1024]{2,1,0:T(2,128)S(1)} %copy.294), channel_id=2, replica_groups=mesh['brick'=8,'grp'=16] {'brick'}, dimensions={0}, use_global_device_ids=true | all-gather | bytes 294912 | tf_op jit(solution)/shard_map/all_gather | solution.py:122
  68.6 19.9 %all-gather.10 = f32[16,4,2]{1,2,0:T(2,128)S(1)} all-gather(f32[1,4,2]{1,2,0:T(2,128)S(1)} %bitcast.616), channel_id=3, replica_groups=mesh['brick'=8,'grp'=16] {'grp'}, dimensions={0}, use_global_device_ids=true | all-gather | bytes 544 | tf_op jit(solution)/shard_map/all_gather | solution.py:189
  94.2 31.1 %all-reduce.18 = f32[32]{0:T(128)S(1)} all-reduce(f32[32]{0:T(128)S(1)} %dynamic-update-slice.3), channel_id=4, replica_groups=mesh['brick'=8,'grp'=16] {'grp'}, use_global_device_ids=true, to_apply=%add.18 | all-reduce | flops 32 | bytes 256 | tf_op jit(solution)/shard_map/triangular_solve/reshape.87 | solution.py:197
  130.3 2.9 cholesky.19
  134.6 2.4 custom-call.14
  153.2 8.4 fusion.46
  167.8 2.4 broadcast_in_dim.696
  171.5 2.4 broadcast_in_dim.702
  184.6 25.6 %all-gather.3 = f32[32,2,1024]{2,1,0:T(2,128)S(1)} all-gather(f32[4,2,1024]{2,1,0:T(2,128)S(1)} %copy.298), channel_id=5, replica_groups=mesh['brick'=8,'grp'=16] {'brick'}, dimensions={0}, use_global_device_ids=true | all-gather | bytes 294912 | tf_op jit(solution)/shard_map/all_gather | solution.py:122
  226.1 3.0 pad_maximum_fusion.2
  231.1 2.4 concatenate.676
  233.6 2.4 concatenate.677
  282.5 3.7 multiply_reduce_fusion.3
  286.2 64.0 %all-reduce.21 = (f32[]{:T(128)}, f32[]{:T(128)}) all-reduce(f32[]{:T(128)} %get-tuple-element.21, f32[]{:T(128)} %get-tuple-element.20), channel_id=1, replica_groups=mesh['brick'=8,'grp'=16] {'brick','grp'}, use_global_device_ids=true, to_apply=%region_16.19 | all-reduce | flops 2 | bytes 16 | tf_op jit(solution)/shard_map/psum | solution.py:213
  362.0 13.5 %all-gather.4 = f32[32,2,1024]{2,1,0:T(2,128)S(1)} all-gather(f32[4,2,1024]{2,1,0:T(2,128)S(1)} %copy.304), channel_id=6, replica_groups=mesh['brick'=8,'grp'=16] {'brick'}, dimensions={0}, use_global_device_ids=true | all-gather | bytes 294912 | tf_op jit(solution)/shard_map/all_gather | solution.py:122
  385.3 9.1 multiply_divide_fusion.1
  400.2 31.6 %all-reduce.19 = f32[32]{0:T(128)} all-reduce(f32[32]{0:T(128)} %dynamic-update-slice.4), channel_id=7, replica_groups=mesh['brick'=8,'grp'=16] {'grp'}, use_global_device_ids=true, to_apply=%add.19 | all-reduce | flops 32 | bytes 256 | tf_op jit(solution)/shard_map/triangular_solve/reshape.87 | solution.py:197
  442.0 3.0 pad_maximum_fusion.4
  447.3 3.0 fusion.96
  487.2 3.7 multiply_reduce_fusion.2
  490.9 71.1 %psum.44 = f32[]{:T(128)} all-reduce(f32[]{:T(128)} %get-tuple-element.54), channel_id=1, replica_groups=mesh['brick'=8,'grp'=16] {'brick','grp'}, use_global_device_ids=true, to_apply=%region_23.26 | all-reduce | flops 1 | bytes 8 | tf_op jit(solution)/shard_map/psum | solution.py:213
  565.9 13.6 %all-gather.6 = f32[32,2,1024]{2,1,0:T(2,128)S(1)} all-gather(f32[4,2,1024]{2,1,0:T(2,128)S(1)} %copy.309), channel_id=8, replica_groups=mesh['brick'=8,'grp'=16] {'brick'}, dimensions={0}, use_global_device_ids=true | all-gather | bytes 294912 | tf_op jit(solution)/shard_map/all_gather | solution.py:122
  588.0 7.3 multiply_add_fusion.1
  603.4 2.7 pad_maximum_fusion.6
  607.5 2.5 broadcast_in_dim.764
  620.1 2.5 concatenate.791
  630.3 2.5 broadcast_in_dim.760
  637.4 3.3 multiply_reduce_fusion.1
  640.7 66.1 %psum.45 = f32[]{:T(128)} all-reduce(f32[]{:T(128)} %get-tuple-element.50), channel_id=1, replica_groups=mesh['brick'=8,'grp'=16] {'brick','grp'}, use_global_device_ids=true, to_apply=%region_26.29 | all-reduce | flops 1 | bytes 8 | tf_op jit(solution)/shard_map/psum | solution.py:213
  711.4 13.5 %all-gather.7 = f32[32,2,1024]{2,1,0:T(2,128)S(1)} all-gather(f32[4,2,1024]{2,1,0:T(2,128)S(1)} %copy.314), channel_id=9, replica_groups=mesh['brick'=8,'grp'=16] {'brick'}, dimensions={0}, use_global_device_ids=true | all-gather | bytes 294912 | tf_op jit(solution)/shard_map/all_gather | solution.py:122
  733.8 8.2 multiply_divide_fusion
  747.8 31.5 %all-reduce.20 = f32[32]{0:T(128)} all-reduce(f32[32]{0:T(128)} %dynamic-update-slice.5), channel_id=10, replica_groups=mesh['brick'=8,'grp'=16] {'grp'}, use_global_device_ids=true, to_apply=%add.20 | all-reduce | flops 32 | bytes 256 | tf_op jit(solution)/shard_map/triangular_solve/reshape.87 | solution.py:197
  788.1 3.0 pad_maximum_fusion.8
  823.6 2.4 broadcast_in_dim.771
  831.9 3.8 multiply_reduce_fusion
  835.8 70.9 %psum.46 = f32[]{:T(128)} all-reduce(f32[]{:T(128)} %get-tuple-element.42), channel_id=1, replica_groups=mesh['brick'=8,'grp'=16] {'brick','grp'}, use_global_device_ids=true, to_apply=%region_30.33 | all-reduce | flops 1 | bytes 8 | tf_op jit(solution)/shard_map/psum | solution.py:213
  914.6 13.8 %all-gather.9 = f32[32,2,1024]{2,1,0:T(2,128)S(1)} all-gather(f32[4,2,1024]{2,1,0:T(2,128)S(1)} %copy.319), channel_id=11, replica_groups=mesh['brick'=8,'grp'=16] {'brick'}, dimensions={0}, use_global_device_ids=true | all-gather | bytes 294912 | tf_op jit(solution)/shard_map/all_gather | solution.py:122
  938.2 10.7 %multiply_add_fusion = f32[2,32,32,32]{3,2,1,0:T(8,128)S(1)} fusion(f32[2,32,32,32]{3,2,1,0:T(8,128)} %copy-done.5, f32[2,32,32,32]{3,2,1,0:T(8,128)} %get-tuple-element.75, f32[2,32,32,32]{3,2,1,0:T(8,128)} %get-tuple-element.77, f32[2,32,32,32]{3,2,1,0:T(8,128)} %get-tuple-element.76, f32[2,32,32,32]{3,2,1,0:T(8,128)} %concatenate.773, ...), kind=kLoop, calls=%fused_computation.76 | loop fusion | flops 3735552 | bytes 5865592 | tf_op jit(solution)/shard_map/add | solution.py:225
  959.3 2.4 broadcast_in_dim.783
  966.9 2.4 concatenate.818
  969.3 2.4 concatenate.775
  978.0 2.5 broadcast_in_dim.779
  984.3 2.6 fusion.155
  988.6 66.6 %psum.47 = f32[]{:T(128)} all-reduce(f32[]{:T(128)} %fusion.155), channel_id=1, replica_groups=mesh['brick'=8,'grp'=16] {'brick','grp'}, use_global_device_ids=true, to_apply=%region_33.36 | all-reduce | flops 1 | bytes 8 | tf_op jit(solution)/shard_map/psum | solution.py:213
  1056.6 6.0 fusion.149
  (713 shorter events, 371.7 us)
Async XLA Ops:
  0.6 9.8 copy-start.37
  0.6 11.2 %copy-start = (f32[1,1,6,2,32,1024]{5,4,3,2,1,0:T(8,128)S(1)}, f32[1,1,6,2,32,1024]{5,4,3,2,1,0:T(8,128)}, u32[]{:S(2)}) copy-start(f32[1,1,6,2,32,1024]{5,4,3,2,1,0:T(8,128)} %param.11) | copy-start | bytes 4718596
  4.7 34.9 %copy-start.95 = (pred[32]{0:T(512)(128)(4,1)}, pred[32]{0:T(512)(128)(4,1)S(1)}, u32[]{:S(2)}) copy-start(pred[32]{0:T(512)(128)(4,1)S(1)} %get-tuple-element.277) | copy-start | bytes 100
  4.7 34.9 %copy-start.101 = (pred[32]{0:T(512)(128)(4,1)}, pred[32]{0:T(512)(128)(4,1)S(1)}, u32[]{:S(2)}) copy-start(pred[32]{0:T(512)(128)(4,1)S(1)} %get-tuple-element.278) | copy-start | bytes 100
  8.2 31.4 %copy-start.85 = (f32[2]{0:T(128)}, f32[2]{0:T(128)S(1)}, u32[]{:S(2)}) copy-start(f32[2]{0:T(128)S(1)} %get-tuple-element.32) | copy-start | bytes 28
  22.2 17.4 %copy-start.118 = (f32[2]{0:T(128)}, f32[2]{0:T(128)S(1)}, u32[]{:S(2)}) copy-start(f32[2]{0:T(128)S(1)} %get-tuple-element.268) | copy-start | bytes 28
  27.9 10.7 %copy-start.20 = (f32[1,1,2,32,1024]{4,3,2,1,0:T(8,128)S(1)}, f32[1,1,2,32,1024]{4,3,2,1,0:T(8,128)}, u32[]{:S(2)}) copy-start(f32[1,1,2,32,1024]{4,3,2,1,0:T(8,128)} %param.9) | copy-start | bytes 786436
  28.0 11.6 %copy-start.38 = (f32[1,1,2,32,1024]{4,3,2,1,0:T(8,128)S(1)}, f32[1,1,2,32,1024]{4,3,2,1,0:T(8,128)}, u32[]{:S(2)}) copy-start(f32[1,1,2,32,1024]{4,3,2,1,0:T(8,128)} %param.10) | copy-start | bytes 786436
  28.0 11.6 %copy-start.122 = (f32[2]{0:T(128)S(1)}, f32[2]{0:T(128)}, u32[]{:S(2)}) copy-start(f32[2]{0:T(128)} %copy-done.121) | copy-start | bytes 28
  28.0 11.6 %copy-start.125 = (f32[2]{0:T(128)S(1)}, f32[2]{0:T(128)}, u32[]{:S(2)}) copy-start(f32[2]{0:T(128)} %copy-done.124) | copy-start | bytes 28
  28.0 11.6 %copy-start.130 = (f32[2]{0:T(128)S(1)}, f32[2]{0:T(128)}, u32[]{:S(2)}) copy-start(f32[2]{0:T(128)} %copy-done.129) | copy-start | bytes 28
  28.0 11.6 %copy-start.134 = (f32[2]{0:T(128)S(1)}, f32[2]{0:T(128)}, u32[]{:S(2)}) copy-start(f32[2]{0:T(128)} %copy-done.133) | copy-start | bytes 28
  28.0 11.6 %copy-start.138 = (f32[2]{0:T(128)S(1)}, f32[2]{0:T(128)}, u32[]{:S(2)}) copy-start(f32[2]{0:T(128)} %copy-done.137) | copy-start | bytes 28
  30.5 121.8 %collective-permute-start.1 = (f32[1,2,1024]{2,1,0:T(2,128)}, f32[1,2,1024]{2,1,0:T(2,128)}, u32[]{:S(2)}, u32[]{:S(2)}) collective-permute-start(f32[1,2,1024]{2,1,0:T(2,128)} %stack_reshape_squeeze.37), channel_id=1, source_target_pairs={{0,1},{1,2},{2,3},{3,4},{4,5},{5,6},{6,7},{7,8},{8,9},{9,10},{10,1... | collective-permute-start | bytes 24584 | tf_op jit(solution)/shard_map/ppermute | solution.py:18
  36.1 115.4 %collective-permute-start = (f32[1,2,1024]{2,1,0:T(2,128)}, f32[1,2,1024]{2,1,0:T(2,128)}, u32[]{:S(2)}, u32[]{:S(2)}) collective-permute-start(f32[1,2,1024]{2,1,0:T(2,128)} %stack_reshape_squeeze.36), channel_id=1, source_target_pairs={{1,0},{2,1},{3,2},{4,3},{5,4},{6,5},{7,6},{8,7},{9,8},{10,9},{11,1... | collective-permute-start | bytes 24584 | tf_op jit(solution)/shard_map/ppermute | solution.py:21
  40.7 19.9 %copy-start.31 = (f32[2,32,1024]{2,1,0:T(8,128)}, f32[2,32,1024]{2,1,0:T(8,128)S(1)}, u32[]{:S(2)}) copy-start(f32[2,32,1024]{2,1,0:T(8,128)S(1)} %get-tuple-element.68) | copy-start | bytes 786436
  40.7 27.0 %copy-start.13 = (f32[2,32,1024]{2,1,0:T(8,128)}, f32[2,32,1024]{2,1,0:T(8,128)S(1)}, u32[]{:S(2)}) copy-start(f32[2,32,1024]{2,1,0:T(8,128)S(1)} %get-tuple-element.73) | copy-start | bytes 786436
  40.7 446.4 %copy-start.11 = (f32[2,32,1024]{2,1,0:T(8,128)}, f32[2,32,1024]{2,1,0:T(8,128)S(1)}, u32[]{:S(2)}) copy-start(f32[2,32,1024]{2,1,0:T(8,128)S(1)} %get-tuple-element.72) | copy-start | bytes 786436
  44.2 16.4 %copy-start.141 = (pred[8,4]{1,0:T(8,128)(4,1)}, pred[8,4]{1,0:T(8,128)(4,1)S(1)}, u32[]{:S(2)}) copy-start(pred[8,4]{1,0:T(8,128)(4,1)S(1)} %iota_compare_fusion.11) | copy-start | bytes 100
  68.2 21.3 %copy-start.7 = (f32[2,32,32,32]{3,2,1,0:T(8,128)S(1)}, f32[2,32,32,32]{3,2,1,0:T(8,128)}, u32[]{:S(2)}) copy-start(f32[2,32,32,32]{3,2,1,0:T(8,128)} %copy-done.6) | copy-start | bytes 786436
  89.5 47.8 %copy-start.59 = (f32[2,32,992]{2,1,0:T(8,128)S(1)}, f32[2,32,992]{2,1,0:T(8,128)}, u32[]{:S(2)}) copy-start(f32[2,32,992]{2,1,0:T(8,128)} %get-tuple-element.146) | copy-start | bytes 761860
  91.3 53.5 %copy-start.96 = (pred[32]{0:T(512)(128)(4,1)S(1)}, pred[32]{0:T(512)(128)(4,1)}, u32[]{:S(2)}) copy-start(pred[32]{0:T(512)(128)(4,1)} %copy-done.95) | copy-start | bytes 100
  91.3 54.2 %copy-start.102 = (pred[32]{0:T(512)(128)(4,1)S(1)}, pred[32]{0:T(512)(128)(4,1)}, u32[]{:S(2)}) copy-start(pred[32]{0:T(512)(128)(4,1)} %copy-done.101) | copy-start | bytes 100
  126.0 22.8 %copy-start.81 = (f32[2,32,32]{2,1,0:T(8,128)}, f32[2,32,32]{2,1,0:T(8,128)S(1)}, u32[]{:S(2)}) copy-start(f32[2,32,32]{2,1,0:T(8,128)S(1)} %reshape.2206) | copy-start | bytes 24580
  126.8 22.1 %copy-start.82 = (f32[2,32,32]{2,1,0:T(8,128)}, f32[2,32,32]{2,1,0:T(8,128)S(1)}, u32[]{:S(2)}) copy-start(f32[2,32,32]{2,1,0:T(8,128)S(1)} %reshape.2205) | copy-start | bytes 24580
  137.4 11.5 %copy-start.57 = (f32[2,31,1024]{2,1,0:T(8,128)S(1)}, f32[2,31,1024]{2,1,0:T(8,128)}, u32[]{:S(2)}) copy-start(f32[2,31,1024]{2,1,0:T(8,128)} %get-tuple-element.142) | copy-start | bytes 761860
  138.6 14.4 %copy-start.156 = (f32[2]{0:T(128)}, f32[2]{0:T(128)S(1)}, u32[]{:S(2)}) copy-start(f32[2]{0:T(128)S(1)} %fusion.180) | copy-start | bytes 28
  221.3 44.6 %collective-permute-start.3 = (f32[1,2,1024]{2,1,0:T(2,128)}, f32[1,2,1024]{2,1,0:T(2,128)}, u32[]{:S(2)}, u32[]{:S(2)}) collective-permute-start(f32[1,2,1024]{2,1,0:T(2,128)} %stack_reshape_squeeze.39), channel_id=1, source_target_pairs={{0,1},{1,2},{2,3},{3,4},{4,5},{5,6},{6,7},{7,8},{8,9},{9,10},{10,1... | collective-permute-start | bytes 24584 | tf_op jit(solution)/shard_map/ppermute | solution.py:18
  223.2 51.0 %collective-permute-start.2 = (f32[1,2,1024]{2,1,0:T(2,128)}, f32[1,2,1024]{2,1,0:T(2,128)}, u32[]{:S(2)}, u32[]{:S(2)}) collective-permute-start(f32[1,2,1024]{2,1,0:T(2,128)} %stack_reshape_squeeze.38), channel_id=1, source_target_pairs={{1,0},{2,1},{3,2},{4,3},{5,4},{6,5},{7,6},{8,7},{9,8},{10,9},{11,1... | collective-permute-start | bytes 24584 | tf_op jit(solution)/shard_map/ppermute | solution.py:21
  359.8 19.8 %copy-start.34 = (f32[2,32,1024]{2,1,0:T(8,128)S(1)}, f32[2,32,1024]{2,1,0:T(8,128)}, u32[]{:S(2)}) copy-start(f32[2,32,1024]{2,1,0:T(8,128)} %copy-done.33) | copy-start | bytes 786436
  436.2 39.2 %collective-permute-start.5 = (f32[1,2,1024]{2,1,0:T(2,128)}, f32[1,2,1024]{2,1,0:T(2,128)}, u32[]{:S(2)}, u32[]{:S(2)}) collective-permute-start(f32[1,2,1024]{2,1,0:T(2,128)} %stack_reshape_squeeze.41), channel_id=1, source_target_pairs={{0,1},{1,2},{2,3},{3,4},{4,5},{5,6},{6,7},{7,8},{8,9},{9,10},{10,1... | collective-permute-start | bytes 24584 | tf_op jit(solution)/shard_map/ppermute | solution.py:18
  438.1 43.2 %collective-permute-start.4 = (f32[1,2,1024]{2,1,0:T(2,128)}, f32[1,2,1024]{2,1,0:T(2,128)}, u32[]{:S(2)}, u32[]{:S(2)}) collective-permute-start(f32[1,2,1024]{2,1,0:T(2,128)} %stack_reshape_squeeze.40), channel_id=1, source_target_pairs={{1,0},{2,1},{3,2},{4,3},{5,4},{6,5},{7,6},{8,7},{9,8},{10,9},{11,1... | collective-permute-start | bytes 24584 | tf_op jit(solution)/shard_map/ppermute | solution.py:21
  599.9 27.8 %collective-permute-start.7 = (f32[1,2,1024]{2,1,0:T(2,128)}, f32[1,2,1024]{2,1,0:T(2,128)}, u32[]{:S(2)}, u32[]{:S(2)}) collective-permute-start(f32[1,2,1024]{2,1,0:T(2,128)} %stack_reshape_squeeze.43), channel_id=1, source_target_pairs={{0,1},{1,2},{2,3},{3,4},{4,5},{5,6},{6,7},{7,8},{8,9},{9,10},{10,1... | collective-permute-start | bytes 24584 | tf_op jit(solution)/shard_map/ppermute | solution.py:18
  602.1 30.7 %collective-permute-start.6 = (f32[1,2,1024]{2,1,0:T(2,128)}, f32[1,2,1024]{2,1,0:T(2,128)}, u32[]{:S(2)}, u32[]{:S(2)}) collective-permute-start(f32[1,2,1024]{2,1,0:T(2,128)} %stack_reshape_squeeze.42), channel_id=1, source_target_pairs={{1,0},{2,1},{3,2},{4,3},{5,4},{6,5},{7,6},{8,7},{9,8},{10,9},{11,1... | collective-permute-start | bytes 24584 | tf_op jit(solution)/shard_map/ppermute | solution.py:21
  607.5 10.3 copy-start.22
  637.4 70.8 %copy-start.45 = (f32[2,32,1024]{2,1,0:T(8,128)S(1)}, f32[2,32,1024]{2,1,0:T(8,128)}, u32[]{:S(2)}) copy-start(f32[2,32,1024]{2,1,0:T(8,128)} %copy-done.44) | copy-start | bytes 786436
  709.7 18.3 %copy-start.54 = (f32[2,32,1024]{2,1,0:T(8,128)}, f32[2,32,1024]{2,1,0:T(8,128)S(1)}, u32[]{:S(2)}) copy-start(f32[2,32,1024]{2,1,0:T(8,128)S(1)} %get-tuple-element.47) | copy-start | bytes 786436
  783.5 36.6 %collective-permute-start.9 = (f32[1,2,1024]{2,1,0:T(2,128)}, f32[1,2,1024]{2,1,0:T(2,128)}, u32[]{:S(2)}, u32[]{:S(2)}) collective-permute-start(f32[1,2,1024]{2,1,0:T(2,128)} %stack_reshape_squeeze.45), channel_id=1, source_target_pairs={{0,1},{1,2},{2,3},{3,4},{4,5},{5,6},{6,7},{7,8},{8,9},{9,10},{10,1... | collective-permute-start | bytes 24584 | tf_op jit(solution)/shard_map/ppermute | solution.py:18
  785.4 40.6 %collective-permute-start.8 = (f32[1,2,1024]{2,1,0:T(2,128)}, f32[1,2,1024]{2,1,0:T(2,128)}, u32[]{:S(2)}, u32[]{:S(2)}) collective-permute-start(f32[1,2,1024]{2,1,0:T(2,128)} %stack_reshape_squeeze.44), channel_id=1, source_target_pairs={{1,0},{2,1},{3,2},{4,3},{5,4},{6,5},{7,6},{8,7},{9,8},{10,9},{11,1... | collective-permute-start | bytes 24584 | tf_op jit(solution)/shard_map/ppermute | solution.py:21
  823.6 8.3 copy-start.108
  823.6 8.3 copy-start.110
  823.6 8.3 copy-start.120
  913.2 19.4 %copy-start.36 = (f32[2,32,1024]{2,1,0:T(8,128)S(1)}, f32[2,32,1024]{2,1,0:T(8,128)}, u32[]{:S(2)}) copy-start(f32[2,32,1024]{2,1,0:T(8,128)} %copy-done.35) | copy-start | bytes 786436
  952.7 22.7 %collective-permute-start.11 = (f32[1,2,1024]{2,1,0:T(2,128)S(1)}, f32[1,2,1024]{2,1,0:T(2,128)S(1)}, u32[]{:S(2)}, u32[]{:S(2)}) collective-permute-start(f32[1,2,1024]{2,1,0:T(2,128)S(1)} %stack_reshape_squeeze.47), channel_id=1, source_target_pairs={{0,1},{1,2},{2,3},{3,4},{4,5},{5,6},{6,7},{7,8},{8,9},{9,10},{10,1... | collective-permute-start | bytes 24584 | tf_op jit(solution)/shard_map/ppermute | solution.py:18
  954.2 26.3 %collective-permute-start.10 = (f32[1,2,1024]{2,1,0:T(2,128)S(1)}, f32[1,2,1024]{2,1,0:T(2,128)S(1)}, u32[]{:S(2)}, u32[]{:S(2)}) collective-permute-start(f32[1,2,1024]{2,1,0:T(2,128)S(1)} %stack_reshape_squeeze.46), channel_id=1, source_target_pairs={{1,0},{2,1},{3,2},{4,3},{5,4},{6,5},{7,6},{8,7},{9,8},{10,9},{11,1... | collective-permute-start | bytes 24584 | tf_op jit(solution)/shard_map/ppermute | solution.py:21
  984.3 72.3 %copy-start.40 = (f32[1,1,2,32,1024]{4,3,2,1,0:T(8,128)S(1)}, f32[1,1,2,32,1024]{4,3,2,1,0:T(8,128)}, u32[]{:S(2)}) copy-start(f32[1,1,2,32,1024]{4,3,2,1,0:T(8,128)} %param.10) | copy-start | bytes 786436
  984.3 72.3 %copy-start.75 = (pred[32,1024]{1,0:T(8,128)(4,1)S(1)}, pred[32,1024]{1,0:T(8,128)(4,1)}, u32[]{:S(2)}) copy-start(pred[32,1024]{1,0:T(8,128)(4,1)} %copy-done.73) | copy-start | bytes 98308
  984.3 72.3 %copy-start.78 = (pred[32,1024]{1,0:T(8,128)(4,1)S(1)}, pred[32,1024]{1,0:T(8,128)(4,1)}, u32[]{:S(2)}) copy-start(pred[32,1024]{1,0:T(8,128)(4,1)} %copy-done.76) | copy-start | bytes 98308
  (131 other events, 441.1 us)
where the time goes:
time: 1080 us; the launch traced here: 1060 us
  blocking collectives  547 us (51%)
  local copies, waits for them, and re-layouts  336 us (31%)
  other arithmetic  139 us (13%)
  starting transfers between devices  22.6 us (2%)
  between operations  15.9 us (1%)
    psum x5, blocking collectives, global_sum(): return lax.psum(jnp.sum(values), ('brick', 'grp'))  339 us
    another operation x3, blocking collectives, coarse_solve(): lax.linalg.triangular_solve(factor, gathered_terms, left_side=True, lower...  94.1 us
    all_gather x6, blocking collectives, apply_operator(): portion = lax.all_gather(outgoing_sides[None], 'brick', axis=0, tiled=True)  94.1 us
    broadcast_in_dim x26, local copies, waits for them, and re-layouts, apply_operator(): jnp.where(cube_third == BS - 1, from_above, jnp.roll(cube, -1, axis=3))  45 us
    broadcast_in_dim x26, local copies, waits for them, and re-layouts, apply_operator(): jnp.where(cube_third == 0, from_below, jnp.roll(cube, 1, axis=3))  43.7 us
    concatenate x12, local copies, waits for them, and re-layouts, apply_operator(): jnp.roll(cube, -1, axis=3)  26.6 us
    concatenate x12, local copies, waits for them, and re-layouts, apply_operator(): jnp.roll(cube, 1, axis=3)  25.4 us
    div x6, other arithmetic, precondition(): smoothed = OMEGA * residual_field / diagonal  24.1 us
  transfers between devices with their start and end apart: 12, of which 0 were waited for; matrix products, arithmetic and copies ran while one was open for 21% of the time, Pallas kernels for 0%

commit v1 on v0

--- a/solution.py
+++ b/solution.py
@@ -119,7 +119,14 @@
                 pad_rows(grid_upper_y[:, PATCH_Y - 1], capacity),
             ]
         )
-        portion = lax.all_gather(outgoing_sides[None], "brick", axis=0, tiled=True)
+        ring = [outgoing_sides[None]]
+        for hop in range(7):
+            ring.append(lax.ppermute(ring[-1], "brick", [(dev, (dev + 1) % 8) for dev in range(8)]))
+        portion = jnp.roll(
+            jnp.concatenate(ring[::-1], axis=0),
+            (lax.axis_index("brick") + 1) * ring[0].shape[0],
+            axis=0,
+        )
         sources = jnp.arange(portion.shape[0], dtype=jnp.int32)
         matches = sources[:, None] == wanted[None, :]
         remote = jnp.zeros((4, capacity, face_size), jnp.float32) + jnp.sum(

time: 1080 us -> 1140 us (1.056)
  blocking collectives: 547 us -> 459 us
  starting transfers between devices: 22.6 us -> 85.1 us
  local copies, waits for them, and re-layouts: 336 us -> 374 us
  waiting for transfers between devices: 0.03 us -> 31.5 us
  other arithmetic: 139 us -> 155 us
    all_gather x6 -> x0, blocking collectives: 94.1 us -> none  [apply_operator(): portion = lax.all_gather(outgoing_sides[None], 'brick', axis=0, tiled=True)]
    ppermute x0 -> x42, starting transfers between devices: none -> 59.1 us  [apply_operator(): lax.ppermute(ring[-1], 'brick', [(dev, (dev + 1) % 8) for dev in range(8)])]
    ppermute x0 -> x42, waiting for transfers between devices: none -> 31.5 us  [apply_operator(): lax.ppermute(ring[-1], 'brick', [(dev, (dev + 1) % 8) for dev in range(8)])]
    unnamed x350 -> x326, local copies, waits for them, and re-layouts: 19.7 us -> 40 us
  transfers between devices with their start and end apart: 12 -> 54, of which waited for: 0 -> 19; matrix products, arithmetic and copies ran while one was open for 21% -> 28% of each run, Pallas kernels for 0% -> 0%
where the time goes in v1:
time: 1140 us; the launch traced here: 1120 us
  blocking collectives  459 us (40%)
  local copies, waits for them, and re-layouts  374 us (33%)
  other arithmetic  155 us (14%)
  starting transfers between devices  85.1 us (7%)
  waiting for transfers between devices  31.5 us (3%)
  between operations  15.5 us (1%)
    psum x5, blocking collectives, global_sum(): return lax.psum(jnp.sum(values), ('brick', 'grp'))  346 us
    another operation x3, blocking collectives, coarse_solve(): lax.linalg.triangular_solve(factor, gathered_terms, left_side=True, lower...  93.1 us
    ppermute x42, starting transfers between devices, apply_operator(): lax.ppermute(ring[-1], 'brick', [(dev, (dev + 1) % 8) for dev in range(8)])  59.1 us
    broadcast_in_dim x26, local copies, waits for them, and re-layouts, apply_operator(): jnp.where(cube_third == BS - 1, from_above, jnp.roll(cube, -1, axis=3))  44.4 us
    broadcast_in_dim x26, local copies, waits for them, and re-layouts, apply_operator(): jnp.where(cube_third == 0, from_below, jnp.roll(cube, 1, axis=3))  41 us
    unnamed x326, local copies, waits for them, and re-layouts  40 us
    ppermute x42, waiting for transfers between devices, apply_operator(): lax.ppermute(ring[-1], 'brick', [(dev, (dev + 1) % 8) for dev in range(8)])  31.5 us
    concatenate x12, local copies, waits for them, and re-layouts, apply_operator(): jnp.roll(cube, -1, axis=3)  26.6 us
  transfers between devices with their start and end apart: 54, of which 19 were waited for; matrix products, arithmetic and copies ran while one was open for 28% of the time, Pallas kernels for 0%

profile of v1, /device:TPU:1, one launch (start us, length us, event | category | flops | bytes accessed | tf_op | source)
XLA Modules:
  0.0 1123.8 jit_solution(7082862433695960275)
XLA Ops:
  5.9 2.6 multiply_divide_fusion.5
  10.8 2.7 collective-permute-start
  22.3 2.5 squeeze.120
  33.4 5.7 multiply_divide_fusion.2
  41.7 4.1 collective-permute-start.8
  57.4 19.9 %all-gather.4 = f32[16,4,2]{1,2,0:T(2,128)S(1)} all-gather(f32[1,4,2]{1,2,0:T(2,128)S(1)} %bitcast.576), channel_id=2, replica_groups=mesh['brick'=8,'grp'=16] {'grp'}, dimensions={0}, use_global_device_ids=true | all-gather | bytes 544 | tf_op jit(solution)/shard_map/all_gather | solution.py:196
  84.8 2.9 cholesky.19
  89.1 2.4 custom-call.14
  93.7 31.7 %all-reduce.18 = f32[32]{0:T(128)S(1)} all-reduce(f32[32]{0:T(128)S(1)} %dynamic-update-slice.3), channel_id=3, replica_groups=mesh['brick'=8,'grp'=16] {'grp'}, use_global_device_ids=true, to_apply=%add.18 | all-reduce | flops 32 | bytes 256 | tf_op jit(solution)/shard_map/triangular_solve/reshape.87 | solution.py:204
  125.4 12.7 %collective-permute-start.1 = (f32[1,4,2,1024]{3,1,2,0:T(4,128)}, f32[1,4,2,1024]{3,1,2,0:T(4,128)S(1)}, u32[]{:S(2)}, u32[]{:S(2)}) collective-permute-start(f32[1,4,2,1024]{3,1,2,0:T(4,128)} %collective-permute-done), channel_id=1, source_target_pairs={{0,16},{16,32},{32,48},{48,64},{64,80},{80,96},{96,112},{112,0},{1... | collective-permute-start | bytes 98312 | tf_op jit(solution)/shard_map/ppermute | solution.py:124
  149.0 2.5 collective-permute-done.4
  152.9 3.4 collective-permute-done.5
  185.3 8.4 fusion.46
  225.5 3.6 collective-permute-done.12
  236.4 3.0 pad_maximum_fusion.2
  245.4 2.4 concatenate.699
  276.3 2.4 broadcast_in_dim.761
  298.2 3.7 multiply_reduce_fusion.3
  301.9 68.6 %all-reduce.21 = (f32[]{:T(128)}, f32[]{:T(128)}) all-reduce(f32[]{:T(128)} %get-tuple-element.18, f32[]{:T(128)} %get-tuple-element.17), channel_id=1, replica_groups=mesh['brick'=8,'grp'=16] {'brick','grp'}, use_global_device_ids=true, to_apply=%region_16.20 | all-reduce | flops 2 | bytes 16 | tf_op jit(solution)/shard_map/psum | solution.py:220
  382.4 8.8 multiply_divide_fusion.1
  406.3 2.7 collective-permute-start.26
  409.0 4.1 fusion.108
  417.0 30.0 %all-reduce.19 = f32[32]{0:T(128)} all-reduce(f32[32]{0:T(128)} %dynamic-update-slice.4), channel_id=4, replica_groups=mesh['brick'=8,'grp'=16] {'grp'}, use_global_device_ids=true, to_apply=%add.19 | all-reduce | flops 32 | bytes 256 | tf_op jit(solution)/shard_map/triangular_solve/reshape.87 | solution.py:204
  447.0 7.7 collective-permute-start.20
  462.0 3.1 pad_maximum_fusion.4
  516.2 3.7 multiply_reduce_fusion.2
  519.9 68.0 %psum.44 = f32[]{:T(128)} all-reduce(f32[]{:T(128)} %get-tuple-element.61), channel_id=1, replica_groups=mesh['brick'=8,'grp'=16] {'brick','grp'}, use_global_device_ids=true, to_apply=%region_23.27 | all-reduce | flops 1 | bytes 8 | tf_op jit(solution)/shard_map/psum | solution.py:220
  603.2 7.3 multiply_add_fusion.1
  618.6 2.6 collective-permute-done.30
  625.0 3.6 collective-permute-start.35
  630.7 2.7 pad_maximum_fusion.6
  641.8 2.5 concatenate.818
  655.4 2.5 broadcast_in_dim.780
  671.5 3.4 multiply_reduce_fusion.1
  674.9 70.2 %psum.45 = f32[]{:T(128)} all-reduce(f32[]{:T(128)} %get-tuple-element.57), channel_id=1, replica_groups=mesh['brick'=8,'grp'=16] {'brick','grp'}, use_global_device_ids=true, to_apply=%region_26.30 | all-reduce | flops 1 | bytes 8 | tf_op jit(solution)/shard_map/psum | solution.py:220
  757.1 8.1 multiply_divide_fusion
  784.4 31.4 %all-reduce.20 = f32[32]{0:T(128)} all-reduce(f32[32]{0:T(128)} %dynamic-update-slice.5), channel_id=5, replica_groups=mesh['brick'=8,'grp'=16] {'grp'}, use_global_device_ids=true, to_apply=%add.20 | all-reduce | flops 32 | bytes 256 | tf_op jit(solution)/shard_map/triangular_solve/reshape.87 | solution.py:204
  815.8 7.2 collective-permute-start.38
  833.7 3.0 pad_maximum_fusion.8
  888.5 3.9 multiply_reduce_fusion
  892.4 68.5 %psum.46 = f32[]{:T(128)} all-reduce(f32[]{:T(128)} %get-tuple-element.49), channel_id=1, replica_groups=mesh['brick'=8,'grp'=16] {'brick','grp'}, use_global_device_ids=true, to_apply=%region_30.34 | all-reduce | flops 1 | bytes 8 | tf_op jit(solution)/shard_map/psum | solution.py:220
  981.7 10.7 multiply_add_fusion
  1003.9 2.8 collective-permute-start.53
  1010.4 3.1 collective-permute-done.50
  1027.8 2.5 broadcast_in_dim.784
  1041.3 2.6 fusion.173
  1044.7 70.2 %psum.47 = f32[]{:T(128)} all-reduce(f32[]{:T(128)} %fusion.173), channel_id=1, replica_groups=mesh['brick'=8,'grp'=16] {'brick','grp'}, use_global_device_ids=true, to_apply=%region_33.37 | all-reduce | flops 1 | bytes 8 | tf_op jit(solution)/shard_map/psum | solution.py:220
  1116.4 6.0 fusion.161
  (766 shorter events, 479.8 us)
Async XLA Ops:
  10.8 114.6 %collective-permute-start = (f32[1,4,2,1024]{3,1,2,0:T(4,128)}, f32[1,4,2,1024]{3,1,2,0:T(4,128)}, u32[]{:S(2)}, u32[]{:S(2)}) collective-permute-start(f32[1,4,2,1024]{3,1,2,0:T(4,128)} %maximum_bitcast_fusion), channel_id=1, source_target_pairs={{0,16},{16,32},{32,48},{48,64},{64,80},{80,96},{96,112},{112,0},{1... | collective-permute-start | bytes 98312 | tf_op jit(solution)/shard_map/ppermute | solution.py:124
  41.7 123.7 %collective-permute-start.8 = (f32[1,2,1024]{2,1,0:T(2,128)}, f32[1,2,1024]{2,1,0:T(2,128)}, u32[]{:S(2)}, u32[]{:S(2)}) collective-permute-start(f32[1,2,1024]{2,1,0:T(2,128)} %stack_reshape_squeeze.37), channel_id=1, source_target_pairs={{0,1},{1,2},{2,3},{3,4},{4,5},{5,6},{6,7},{7,8},{8,9},{9,10},{10,1... | collective-permute-start | bytes 24584 | tf_op jit(solution)/shard_map/ppermute | solution.py:18
  46.5 116.6 %collective-permute-start.7 = (f32[1,2,1024]{2,1,0:T(2,128)}, f32[1,2,1024]{2,1,0:T(2,128)}, u32[]{:S(2)}, u32[]{:S(2)}) collective-permute-start(f32[1,2,1024]{2,1,0:T(2,128)} %stack_reshape_squeeze.36), channel_id=1, source_target_pairs={{1,0},{2,1},{3,2},{4,3},{5,4},{6,5},{7,6},{8,7},{9,8},{10,9},{11,1... | collective-permute-start | bytes 24584 | tf_op jit(solution)/shard_map/ppermute | solution.py:21
  125.4 14.1 %collective-permute-start.1 = (f32[1,4,2,1024]{3,1,2,0:T(4,128)}, f32[1,4,2,1024]{3,1,2,0:T(4,128)S(1)}, u32[]{:S(2)}, u32[]{:S(2)}) collective-permute-start(f32[1,4,2,1024]{3,1,2,0:T(4,128)} %collective-permute-done), channel_id=1, source_target_pairs={{0,16},{16,32},{32,48},{48,64},{64,80},{80,96},{96,112},{112,0},{1... | collective-permute-start | bytes 98312 | tf_op jit(solution)/shard_map/ppermute | solution.py:124
  142.7 6.2 collective-permute-start.3
  151.6 4.7 collective-permute-start.5
  156.2 15.2 %collective-permute-start.6 = (f32[1,4,2,1024]{3,1,2,0:T(4,128)}, f32[1,4,2,1024]{3,1,2,0:T(4,128)}, u32[]{:S(2)}, u32[]{:S(2)}) collective-permute-start(f32[1,4,2,1024]{3,1,2,0:T(4,128)} %collective-permute-done.5), channel_id=1, source_target_pairs={{0,16},{16,32},{32,48},{48,64},{64,80},{80,96},{96,112},{112,0},{1... | collective-permute-start | bytes 98312 | tf_op jit(solution)/shard_map/ppermute | solution.py:124
  210.3 4.9 collective-permute-start.9
  215.2 4.7 collective-permute-start.10
  219.9 4.6 collective-permute-start.11
  224.5 4.7 collective-permute-start.12
  229.1 7.3 collective-permute-start.13
  233.1 31.4 %collective-permute-start.17 = (f32[1,2,1024]{2,1,0:T(2,128)}, f32[1,2,1024]{2,1,0:T(2,128)}, u32[]{:S(2)}, u32[]{:S(2)}) collective-permute-start(f32[1,2,1024]{2,1,0:T(2,128)} %stack_reshape_squeeze.39), channel_id=1, source_target_pairs={{0,1},{1,2},{2,3},{3,4},{4,5},{5,6},{6,7},{7,8},{8,9},{9,10},{10,1... | collective-permute-start | bytes 24584 | tf_op jit(solution)/shard_map/ppermute | solution.py:18
  234.9 37.9 %collective-permute-start.16 = (f32[1,2,1024]{2,1,0:T(2,128)}, f32[1,2,1024]{2,1,0:T(2,128)}, u32[]{:S(2)}, u32[]{:S(2)}) collective-permute-start(f32[1,2,1024]{2,1,0:T(2,128)} %stack_reshape_squeeze.38), channel_id=1, source_target_pairs={{1,0},{2,1},{3,2},{4,3},{5,4},{6,5},{7,6},{8,7},{9,8},{10,9},{11,1... | collective-permute-start | bytes 24584 | tf_op jit(solution)/shard_map/ppermute | solution.py:21
  236.4 4.9 collective-permute-start.14
  241.3 39.8 %collective-permute-start.15 = (f32[1,4,2,1024]{3,1,2,0:T(4,128)}, f32[1,4,2,1024]{3,1,2,0:T(4,128)}, u32[]{:S(2)}, u32[]{:S(2)}) collective-permute-start(f32[1,4,2,1024]{3,1,2,0:T(4,128)} %collective-permute-done.14), channel_id=1, source_target_pairs={{0,16},{16,32},{32,48},{48,64},{64,80},{80,96},{96,112},{112,0},{1... | collective-permute-start | bytes 98312 | tf_op jit(solution)/shard_map/ppermute | solution.py:124
  403.2 11.0 collective-permute-start.18
  406.3 79.0 %collective-permute-start.26 = (f32[1,2,1024]{2,1,0:T(2,128)}, f32[1,2,1024]{2,1,0:T(2,128)}, u32[]{:S(2)}, u32[]{:S(2)}) collective-permute-start(f32[1,2,1024]{2,1,0:T(2,128)} %stack_reshape_squeeze.41), channel_id=1, source_target_pairs={{0,1},{1,2},{2,3},{3,4},{4,5},{5,6},{6,7},{7,8},{8,9},{9,10},{10,1... | collective-permute-start | bytes 24584 | tf_op jit(solution)/shard_map/ppermute | solution.py:18
  414.2 32.8 %collective-permute-start.19 = (f32[1,4,2,1024]{3,1,2,0:T(4,128)}, f32[1,4,2,1024]{3,1,2,0:T(4,128)}, u32[]{:S(2)}, u32[]{:S(2)}) collective-permute-start(f32[1,4,2,1024]{3,1,2,0:T(4,128)} %collective-permute-done.18), channel_id=1, source_target_pairs={{0,16},{16,32},{32,48},{48,64},{64,80},{80,96},{96,112},{112,0},{1... | collective-permute-start | bytes 98312 | tf_op jit(solution)/shard_map/ppermute | solution.py:124
  447.0 9.0 collective-permute-start.20
  456.0 5.9 collective-permute-start.21
  460.4 33.2 %collective-permute-start.25 = (f32[1,2,1024]{2,1,0:T(2,128)}, f32[1,2,1024]{2,1,0:T(2,128)}, u32[]{:S(2)}, u32[]{:S(2)}) collective-permute-start(f32[1,2,1024]{2,1,0:T(2,128)} %stack_reshape_squeeze.40), channel_id=1, source_target_pairs={{1,0},{2,1},{3,2},{4,3},{5,4},{6,5},{7,6},{8,7},{9,8},{10,9},{11,1... | collective-permute-start | bytes 24584 | tf_op jit(solution)/shard_map/ppermute | solution.py:21
  465.2 4.7 collective-permute-start.23
  469.9 32.1 %collective-permute-start.24 = (f32[1,4,2,1024]{3,1,2,0:T(4,128)}, f32[1,4,2,1024]{3,1,2,0:T(4,128)}, u32[]{:S(2)}, u32[]{:S(2)}) collective-permute-start(f32[1,4,2,1024]{3,1,2,0:T(4,128)} %collective-permute-done.23), channel_id=1, source_target_pairs={{0,16},{16,32},{32,48},{48,64},{64,80},{80,96},{96,112},{112,0},{1... | collective-permute-start | bytes 98312 | tf_op jit(solution)/shard_map/ppermute | solution.py:124
  598.1 12.5 %collective-permute-start.27 = (f32[1,4,2,1024]{3,1,2,0:T(4,128)}, f32[1,4,2,1024]{3,1,2,0:T(4,128)}, u32[]{:S(2)}, u32[]{:S(2)}) collective-permute-start(f32[1,4,2,1024]{3,1,2,0:T(4,128)} %maximum_bitcast_fusion.3), channel_id=1, source_target_pairs={{0,16},{16,32},{32,48},{48,64},{64,80},{80,96},{96,112},{112,0},{1... | collective-permute-start | bytes 98312 | tf_op jit(solution)/shard_map/ppermute | solution.py:124
  612.0 4.5 collective-permute-start.29
  616.5 4.7 collective-permute-start.30
  621.2 9.2 collective-permute-start.31
  625.0 24.1 %collective-permute-start.35 = (f32[1,2,1024]{2,1,0:T(2,128)}, f32[1,2,1024]{2,1,0:T(2,128)}, u32[]{:S(2)}, u32[]{:S(2)}) collective-permute-start(f32[1,2,1024]{2,1,0:T(2,128)} %stack_reshape_squeeze.43), channel_id=1, source_target_pairs={{0,1},{1,2},{2,3},{3,4},{4,5},{5,6},{6,7},{7,8},{8,9},{9,10},{10,1... | collective-permute-start | bytes 24584 | tf_op jit(solution)/shard_map/ppermute | solution.py:18
  628.6 24.0 %collective-permute-start.34 = (f32[1,2,1024]{2,1,0:T(2,128)}, f32[1,2,1024]{2,1,0:T(2,128)}, u32[]{:S(2)}, u32[]{:S(2)}) collective-permute-start(f32[1,2,1024]{2,1,0:T(2,128)} %stack_reshape_squeeze.42), channel_id=1, source_target_pairs={{1,0},{2,1},{3,2},{4,3},{5,4},{6,5},{7,6},{8,7},{9,8},{10,9},{11,1... | collective-permute-start | bytes 24584 | tf_op jit(solution)/shard_map/ppermute | solution.py:21
  630.4 4.9 collective-permute-start.32
  635.3 25.0 %collective-permute-start.33 = (f32[1,4,2,1024]{3,1,2,0:T(4,128)}, f32[1,4,2,1024]{3,1,2,0:T(4,128)}, u32[]{:S(2)}, u32[]{:S(2)}) collective-permute-start(f32[1,4,2,1024]{3,1,2,0:T(4,128)} %collective-permute-done.32), channel_id=1, source_target_pairs={{0,16},{16,32},{32,48},{48,64},{64,80},{80,96},{96,112},{112,0},{1... | collective-permute-start | bytes 98312 | tf_op jit(solution)/shard_map/ppermute | solution.py:124
  776.8 3.3 collective-permute-start.36
  780.1 35.7 %collective-permute-start.37 = (f32[1,4,2,1024]{3,1,2,0:T(4,128)}, f32[1,4,2,1024]{3,1,2,0:T(4,128)}, u32[]{:S(2)}, u32[]{:S(2)}) collective-permute-start(f32[1,4,2,1024]{3,1,2,0:T(4,128)} %collective-permute-done.36), channel_id=1, source_target_pairs={{0,16},{16,32},{32,48},{48,64},{64,80},{80,96},{96,112},{112,0},{1... | collective-permute-start | bytes 98312 | tf_op jit(solution)/shard_map/ppermute | solution.py:124
  815.8 9.1 collective-permute-start.38
  824.9 8.8 collective-permute-start.39
  830.3 27.3 %collective-permute-start.44 = (f32[1,2,1024]{2,1,0:T(2,128)}, f32[1,2,1024]{2,1,0:T(2,128)}, u32[]{:S(2)}, u32[]{:S(2)}) collective-permute-start(f32[1,2,1024]{2,1,0:T(2,128)} %stack_reshape_squeeze.45), channel_id=1, source_target_pairs={{0,1},{1,2},{2,3},{3,4},{4,5},{5,6},{6,7},{7,8},{8,9},{9,10},{10,1... | collective-permute-start | bytes 24584 | tf_op jit(solution)/shard_map/ppermute | solution.py:18
  832.2 33.7 %collective-permute-start.43 = (f32[1,2,1024]{2,1,0:T(2,128)}, f32[1,2,1024]{2,1,0:T(2,128)}, u32[]{:S(2)}, u32[]{:S(2)}) collective-permute-start(f32[1,2,1024]{2,1,0:T(2,128)} %stack_reshape_squeeze.44), channel_id=1, source_target_pairs={{1,0},{2,1},{3,2},{4,3},{5,4},{6,5},{7,6},{8,7},{9,8},{10,9},{11,1... | collective-permute-start | bytes 24584 | tf_op jit(solution)/shard_map/ppermute | solution.py:21
  836.7 4.6 collective-permute-start.41
  841.3 32.9 %collective-permute-start.42 = (f32[1,4,2,1024]{3,1,2,0:T(4,128)}, f32[1,4,2,1024]{3,1,2,0:T(4,128)}, u32[]{:S(2)}, u32[]{:S(2)}) collective-permute-start(f32[1,4,2,1024]{3,1,2,0:T(4,128)} %collective-permute-done.41), channel_id=1, source_target_pairs={{0,16},{16,32},{32,48},{48,64},{64,80},{80,96},{96,112},{112,0},{1... | collective-permute-start | bytes 98312 | tf_op jit(solution)/shard_map/ppermute | solution.py:124
  975.5 17.0 %collective-permute-start.45 = (f32[1,4,2,1024]{3,1,2,0:T(4,128)}, f32[1,4,2,1024]{3,1,2,0:T(4,128)}, u32[]{:S(2)}, u32[]{:S(2)}) collective-permute-start(f32[1,4,2,1024]{3,1,2,0:T(4,128)} %maximum_bitcast_fusion.5), channel_id=1, source_target_pairs={{0,16},{16,32},{32,48},{48,64},{64,80},{80,96},{96,112},{112,0},{1... | collective-permute-start | bytes 98312 | tf_op jit(solution)/shard_map/ppermute | solution.py:124
  994.2 3.7 collective-permute-start.47
  997.9 3.5 collective-permute-start.48
  1001.5 6.8 collective-permute-start.49
  1003.9 19.6 %collective-permute-start.53 = (f32[1,2,1024]{2,1,0:T(2,128)S(1)}, f32[1,2,1024]{2,1,0:T(2,128)S(1)}, u32[]{:S(2)}, u32[]{:S(2)}) collective-permute-start(f32[1,2,1024]{2,1,0:T(2,128)S(1)} %stack_reshape_squeeze.47), channel_id=1, source_target_pairs={{0,1},{1,2},{2,3},{3,4},{4,5},{5,6},{6,7},{7,8},{8,9},{9,10},{10,1... | collective-permute-start | bytes 24584 | tf_op jit(solution)/shard_map/ppermute | solution.py:18
  1006.7 19.6 %collective-permute-start.52 = (f32[1,2,1024]{2,1,0:T(2,128)S(1)}, f32[1,2,1024]{2,1,0:T(2,128)S(1)}, u32[]{:S(2)}, u32[]{:S(2)}) collective-permute-start(f32[1,2,1024]{2,1,0:T(2,128)S(1)} %stack_reshape_squeeze.46), channel_id=1, source_target_pairs={{1,0},{2,1},{3,2},{4,3},{5,4},{6,5},{7,6},{8,7},{9,8},{10,9},{11,1... | collective-permute-start | bytes 24584 | tf_op jit(solution)/shard_map/ppermute | solution.py:21
  1008.3 5.2 collective-permute-start.50
  1013.5 19.2 %collective-permute-start.51 = (f32[1,4,2,1024]{3,1,2,0:T(4,128)}, f32[1,4,2,1024]{3,1,2,0:T(4,128)}, u32[]{:S(2)}, u32[]{:S(2)}) collective-permute-start(f32[1,4,2,1024]{3,1,2,0:T(4,128)} %collective-permute-done.50), channel_id=1, source_target_pairs={{0,16},{16,32},{32,48},{48,64},{64,80},{80,96},{96,112},{112,0},{1... | collective-permute-start | bytes 98312 | tf_op jit(solution)/shard_map/ppermute | solution.py:124
  (146 other events, 2100.1 us)
